TPU v7x, 256 devices: a whole 4x4x8 slice. The times are simulated.
256 devices in a mesh: env: 4 (over x_lo, core), tm: 64 (over x_hi, z, y).
Axes of the slice: x: 4 (x_hi: 2, x_lo: 2; x = x_hi * 2 + x_lo), y: 4, z: 8, core: 2. Of those that a mesh axis runs over, the one named last changes fastest.
Arguments:
- hidden: bfloat16 [4, 64, 256, 1024], P('env', 'tm'), may hold values from -6 to 6
- done_step: int32 [4, 64], P('env', 'tm'), may hold values from 0 to 255
- alive: int32 [4, 64, 256], P('env', None, 'tm'), may hold values 0 or 1
- targets: float32 [4, 64, 256], P('env', None, 'tm'), may hold values from -6 to 6
- gain_t: float32 [1024], replicated, may hold values from 0.25 to 1.75
- w_qkv_t: bfloat16 [1024, 3072], replicated, may hold values from -5 to 5
- w_out_t: bfloat16 [1024, 1024], replicated, may hold values from -0.1875 to 0.1875
- gain_a: float32 [1024], replicated, may hold values from 0.25 to 1.75
- w_qkv_a: bfloat16 [1024, 3072], P('tm'), may hold values from -5 to 5
- w_out_a: bfloat16 [1024, 1024], P('tm'), may hold values from -0.1875 to 0.1875
- w_value: float32 [1024], replicated, may hold values from -0.1875 to 0.1875
Outputs:
- values: float32 [4, 64, 256], P('env', None, 'tm')
- input_grad: bfloat16 [4, 64, 256, 1024], P('env', 'tm')
- qkv_grad: float32 [1024, 3072], P('tm')
- out_grad: float32 [1024, 1024], P('tm')
Inputs may be any that keep to these rules, and one draw needn't show every extreme that they name: `done_step`: the last step of an agent's first episode in the window; later steps form a new episode.
All inputs are finite; a program needn't handle non-finite values. No bound on the sum of `alive` on one device may be relied on, other than what follows from the above.
Results may differ from a plain program's by a relative error of at most 0.02.
Values may be sent and summed in bfloat16 or wider, within the bound.
A program may use at most 128 MiB of HBM per device.

v0:
```python
import math
import jax
import jax.numpy as jnp
from jax import lax
from jax.sharding import PartitionSpec as P

HEADS = 8
HI = lax.Precision.HIGHEST


def norm_scale(rows, gain):
    return rows * lax.rsqrt(jnp.mean(rows * rows, axis=-1, keepdims=True) + 1e-06) * gain


def attend(qkv, allowed, head_count):
    width = qkv.shape[-1] // 3
    size = width // head_count
    shape = qkv.shape[:-1] + (head_count, size)
    queries = qkv[..., :width].reshape(shape)
    key_rows = qkv[..., width : 2 * width].reshape(shape)
    value_rows = qkv[..., 2 * width :].reshape(shape)
    scores = jnp.einsum("qhe,khe->hqk", queries, key_rows, preferred_element_type=jnp.float32)
    scores = jnp.where(allowed[None], scores / math.sqrt(size), -1e30)
    row_max = jnp.max(scores, axis=-1, keepdims=True)
    weights = jnp.exp(scores - row_max)
    probs = (weights / jnp.sum(weights, axis=-1, keepdims=True)).astype(jnp.bfloat16)
    mixed = jnp.einsum("hqk,khe->qhe", probs, value_rows, preferred_element_type=jnp.float32)
    return mixed.reshape(qkv.shape[:-1] + (width,))


def temporal_block(rows, done, gain, w_qkv, w_out, head_count):
    length, width = rows.shape
    rows_f = rows.astype(jnp.float32)
    normed = norm_scale(rows_f, gain).astype(jnp.bfloat16)
    qkv = jnp.dot(normed, w_qkv, preferred_element_type=jnp.float32).astype(jnp.bfloat16)
    positions = jnp.arange(length, dtype=jnp.int32)
    later = positions > done
    allowed = (positions[:, None] >= positions[None, :]) & (later[:, None] == later[None, :])
    mixed = attend(qkv, allowed, head_count).astype(jnp.bfloat16)
    added = jnp.dot(mixed, w_out, preferred_element_type=jnp.float32)
    return (rows_f + added).astype(jnp.bfloat16)


def left_product(left, right):
    return lax.dot_general(
        left, right, (((0,), (0,)), ((), ())), preferred_element_type=jnp.float32
    )


def agent_step(lifted, alive_rows, target_rows, gain, w_qk, z, w_value, head_count):
    agent_count, step_count, width = lifted.shape
    size = width // head_count
    lifted_f = lifted.astype(jnp.float32)
    normed_f, norm_pull = jax.vjp(lambda rows: norm_scale(rows, gain), lifted_f)
    normed = normed_f.astype(jnp.bfloat16).reshape(-1, width)
    qk = jnp.dot(normed, w_qk, preferred_element_type=jnp.float32).astype(jnp.bfloat16)
    qk = qk.reshape(agent_count, step_count, 2, head_count, size)
    q, k = (qk[:, :, 0], qk[:, :, 1])
    s = jnp.dot(normed.astype(jnp.float32), z, precision=HI)
    s = s.reshape(agent_count, step_count, head_count).transpose(1, 2, 0)
    living = alive_rows.T == 1
    allowed = living[:, None, :] | jnp.eye(agent_count, dtype=bool)[None]
    scores = jnp.einsum("qbhe,kbhe->bhqk", q, k, preferred_element_type=jnp.float32)
    scores = jnp.where(allowed[:, None], scores / math.sqrt(size), -1e30)
    weights = jnp.exp(scores - jnp.max(scores, axis=-1, keepdims=True))
    probs = weights / jnp.sum(weights, axis=-1, keepdims=True)
    pv = jnp.sum(probs * s[:, :, None, :], axis=-1)
    predicted = jnp.sum(lifted_f * w_value, axis=-1) + jnp.sum(pv, axis=1).T
    err = 32.0 * alive_rows.astype(jnp.float32) * (predicted - target_rows)
    weighted = probs * err.T[:, None, :, None]
    t = jnp.sum(weighted, axis=2)
    ds = weighted * (s[:, :, None, :] - pv[..., None]) * (1.0 / math.sqrt(size))
    ds = ds.astype(jnp.bfloat16)
    dq = jnp.einsum("bhqk,kbhe->qbhe", ds, k, preferred_element_type=jnp.float32)
    dk = jnp.einsum("bhqk,qbhe->kbhe", ds, q, preferred_element_type=jnp.float32)
    dqk = jnp.stack([dq, dk], axis=2).astype(jnp.bfloat16).reshape(-1, 2 * width)
    t = t.transpose(2, 0, 1).reshape(-1, head_count)
    grad_normed = jnp.dot(dqk, w_qk.T, preferred_element_type=jnp.float32)
    grad_normed = grad_normed + jnp.dot(t, z.T, precision=HI)
    grad_top = err[..., None] * w_value
    grad_lifted = grad_top + norm_pull(grad_normed.reshape(agent_count, step_count, width))[0]
    return (predicted, grad_lifted.astype(jnp.bfloat16), normed, dqk, t)


def per_device(
    hidden, done_step, alive, targets, gain_t, w_qkv_t, w_out_t, gain_a, w_qkv_a, w_out_a, w_value
):
    width = hidden.shape[-1]
    size = width // HEADS
    local_rows = hidden[0, 0]
    done = done_step[0, 0]
    v = lax.all_gather(
        jnp.sum(w_out_a.astype(jnp.float32) * w_value, axis=1), "tm", axis=0, tiled=True
    )
    w_v = w_qkv_a[:, 2 * width :].astype(jnp.float32)
    z = jnp.sum((w_v * v).reshape(-1, HEADS, size), axis=-1)
    z = lax.all_gather(z, "tm", axis=0, tiled=True)
    w_qk = lax.all_gather(w_qkv_a[:, : 2 * width], "tm", axis=0, tiled=True)
    first, pull = jax.vjp(
        lambda rows: temporal_block(rows, done, gain_t, w_qkv_t, w_out_t, HEADS), local_rows
    )
    lifted = lax.all_to_all(first[None], "tm", split_axis=1, concat_axis=0, tiled=True)
    predicted, grad_lifted, normed, dqk, t = agent_step(
        lifted, alive[0], targets[0], gain_a, w_qk, z, w_value, HEADS
    )
    returned = lax.all_to_all(grad_lifted, "tm", split_axis=0, concat_axis=1, tiled=True)
    terms = left_product(normed, dqk).astype(jnp.bfloat16)
    u_terms = lax.dot_general(normed.astype(jnp.float32), t, (((0,), (0,)), ((), ())), precision=HI)
    summed = lax.psum_scatter(terms, "tm", scatter_dimension=0, tiled=True)
    qk_grad = lax.psum(summed, "env").astype(jnp.float32)
    u_mine = lax.psum(u_terms, ("env", "tm"))
    u_mine = lax.dynamic_slice_in_dim(u_mine, lax.axis_index("tm") * w_v.shape[0], w_v.shape[0], 0)
    u_wide = jnp.repeat(u_mine, size, axis=1)
    v_grad = u_wide * v
    mixed_err = lax.psum(jnp.sum(u_wide * w_v, axis=0), "tm")
    mixed_err = lax.dynamic_slice_in_dim(
        mixed_err, lax.axis_index("tm") * w_out_a.shape[0], w_out_a.shape[0], 0
    )
    out_grad = mixed_err[:, None] * w_value
    qkv_grad = jnp.concatenate([qk_grad, v_grad], axis=1)
    input_grad = pull(returned[0])[0]
    return (predicted[None], input_grad[None, None], qkv_grad, out_grad)


def solution(mesh):
    in_specs = (
        P("env", "tm", None, None),
        P("env", "tm"),
        P("env", None, "tm"),
        P("env", None, "tm"),
        P(),
        P(),
        P(),
        P(),
        P("tm", None),
        P("tm", None),
        P(),
    )
    out_specs = (P("env", None, "tm"), P("env", "tm", None, None), P("tm", None), P("tm", None))
    return jax.shard_map(
        per_device, mesh=mesh, in_specs=in_specs, out_specs=out_specs, check_vma=False
    )
```

profile of v0, /device:TPU:1, one launch (start us, length us, event | category | flops | bytes accessed | tf_op | source)
XLA Modules:
  0.0 856.8 jit_solution(7488116643575696525)
XLA Ops:
  7.2 1.6 slice.24
  9.5 1.2 fusion.49
  10.7 0.5 copy-done.25
  11.3 4.9 convolution_convert_fusion
  16.1 1.1 slice_bitcast_fusion
  17.2 1.4 copy.98
  18.7 2.2 copy.97
  21.0 1.6 fusion.114
  23.3 0.7 copy-done.1
  24.0 1.0 copy-done.3
  25.4 0.7 fusion.37
  26.1 0.8 copy.135
  27.0 0.5 broadcast.202
  27.5 4.5 reduce.4
  32.0 2.2 reshape.279
  34.2 15.1 %all-to-all-start = ((bf16[64,2,2048]{2,1,0:T(2,128)(2,1)}), bf16[64,2,2048]{2,1,0:T(2,128)(2,1)S(1)}, u32[]{:S(2)}, u32[]{:S(2)}) async-start(bf16[64,2,2048]{2,1,0:T(2,128)(2,1)} %reshape.279), calls=%async_computation | async-start | bytes 1048576 | tf_op jit(solution)/shard_map/all_to_all | solution.py:102
  49.4 0.6 dynamic-slice
  51.0 156.9 %all-reduce.3 = f32[1024]{0:T(1024)S(1)} all-reduce(f32[1024]{0:T(1024)S(1)} %dynamic-update-slice), channel_id=1, replica_groups=mesh['env'=4,'tm'=64] {'tm'}, use_global_device_ids=true, to_apply=%add.3 | all-reduce | flops 1024 | bytes 8192
  207.9 0.8 fusion.93
  208.9 148.0 %all-gather = f32[64,16,8]{1,2,0:T(8,128)S(1)} all-gather(f32[1,16,8]{1,2,0:T(8,128)S(1)} %bitcast.169), channel_id=1, replica_groups=mesh['env'=4,'tm'=64] {'tm'}, dimensions={0}, use_global_device_ids=true | all-gather | bytes 33280 | tf_op jit(solution)/shard_map/all_gather | solution.py:97
  357.2 0.7 broadcast_or_fusion
  357.9 1.8 reshape.280
  359.7 1.6 fusion.39
  361.5 0.7 copy.75
  362.2 1.3 reshape.268
  363.5 1.5 multiply_convert_fusion
  365.0 0.8 copy-done.6
  365.8 1.3 convolution_bitcast_fusion.3
  367.1 3.5 fusion.16
  370.9 1.0 fusion.113
  371.9 3.5 multiply_reduce_fusion.2
  375.4 1.3 fusion.95
  376.7 3.3 convolution_bitcast_fusion
  380.0 3.4 convolution_bitcast_fusion.1
  383.5 1.3 maximum_convert_fusion
  384.8 1.7 copy.78
  386.4 2.3 convert_element_type.173
  388.7 4.6 convolution_convert_fusion.1
  393.5 0.5 copy-done.22
  394.1 1.6 multiply_reduce_fusion
  395.8 3.8 fusion.115
  399.6 2.1 fusion.40
  401.8 2.6 reshape.260
  404.4 2.8 fusion.47
  407.2 4.9 all-to-all-start.1
  412.1 1.5 convolution_bitcast_fusion.2
  413.6 132.2 %psum.22 = f32[1024,8]{0,1:T(8,128)S(1)} all-reduce(f32[1024,8]{0,1:T(8,128)S(1)} %convolution_bitcast_fusion.2), channel_id=1, replica_groups=mesh['env'=4,'tm'=64] {'env','tm'}, use_global_device_ids=true, to_apply=%region_19.20 | all-reduce | flops 8192 | bytes 65536 | tf_op jit(solution)/shard_map/psum | solution.py:111
  546.0 0.8 fusion.94
  546.8 156.0 %psum.23 = f32[1024]{0:T(1024)S(1)} all-reduce(f32[1024]{0:T(1024)S(1)} %get-tuple-element.19), channel_id=1, replica_groups=mesh['env'=4,'tm'=64] {'tm'}, use_global_device_ids=true, to_apply=%region_21.22 | all-reduce | flops 1024 | bytes 8192 | tf_op jit(solution)/shard_map/psum | solution.py:115
  702.9 0.7 broadcast_multiply_fusion
  703.6 0.9 squeeze.21
  704.6 2.6 convolution_convert_fusion.5
  707.2 1.2 copy.94
  708.5 2.3 fusion.6
  710.9 1.0 convert_reduce_fusion
  712.6 1.2 fusion.25
  713.8 1.2 fusion.24
  715.2 0.7 slice-done.1
  716.0 2.9 fusion.52
  718.9 45.1 %reduce-scatter.2.cloned.1.call-done = bf16[16,2048]{1,0:T(8,128)(2,1)} async-done(((bf16[1024,2048]{1,0:T(8,128)(2,1)}), bf16[16,2048]{1,0:T(8,128)(2,1)}) %reduce-scatter.2.cloned.1.call-update) | async-done | bytes 65552 | tf_op jit(solution)/shard_map/reduce_scatter | solution.py:109
  764.1 2.3 fusion.67
  766.4 82.4 %all-reduce.6.cloned.1.call-done = bf16[16,2048]{1,0:T(8,128)(2,1)} async-done(((bf16[16,2048]{1,0:T(8,128)(2,1)}), bf16[16,2048]{1,0:T(8,128)(2,1)}) %all-reduce.6.cloned.1.call-update) | async-done | bytes 65552 | tf_op jit(solution)/shard_map/psum | solution.py:110
  848.8 0.8 convert_element_type.192
  849.6 0.7 pad_maximum_fusion
  (107 shorter events, 4.4 us)
Async XLA Ops:
  7.2 18.2 %copy-start = (bf16[1024,1024]{1,0:T(8,128)(2,1)S(1)}, bf16[1024,1024]{1,0:T(8,128)(2,1)}, u32[]{:S(2)}) copy-start(bf16[1024,1024]{1,0:T(8,128)(2,1)} %param.17) | copy-start | bytes 6291460
  7.2 359.9 %all-gather.3.cloned.1.call-start = ((), (), s32[]{:S(2)}) async-start(), calls=%async_computation.3 | async-start | bytes 4259840 | tf_op jit(solution)/shard_map/all_gather | solution.py:98
  10.7 0.5 copy-start.25
  11.3 4.9 copy-start.28
  17.2 6.8 copy-start.9
  18.7 3.9 copy-start.11
  22.6 1.4 copy-start.1
  22.9 2.4 copy-start.16
  22.9 2.4 copy-start.7
  24.0 1.0 copy-start.3
  26.9 22.4 %copy-start.31 = (u32[256]{0:T(256)S(1)}, u32[256]{0:T(256)}, u32[]{:S(2)}) copy-start(u32[256]{0:T(256)} %constant.61) | copy-start | bytes 3076
  26.9 23.7 %copy-start.18 = (f32[1024]{0:T(1024)S(1)}, f32[1024]{0:T(1024)}, u32[]{:S(2)}) copy-start(f32[1024]{0:T(1024)} %param.21) | copy-start | bytes 12292
  27.0 23.7 %copy-start.21 = (bf16[16,1024]{1,0:T(8,128)(2,1)S(1)}, bf16[16,1024]{1,0:T(8,128)(2,1)}, u32[]{:S(2)}) copy-start(bf16[16,1024]{1,0:T(8,128)(2,1)} %param.20) | copy-start | bytes 98308
  32.0 325.1 %copy-start.27 = (s32[1,64,4]{1,2,0:T(4,128)S(1)}, s32[1,64,4]{1,2,0:T(4,128)}, u32[]{:S(2)}) copy-start(s32[1,64,4]{1,2,0:T(4,128)} %param.13) | copy-start | bytes 3076
  34.2 323.7 %all-to-all-start = ((bf16[64,2,2048]{2,1,0:T(2,128)(2,1)}), bf16[64,2,2048]{2,1,0:T(2,128)(2,1)S(1)}, u32[]{:S(2)}, u32[]{:S(2)}) async-start(bf16[64,2,2048]{2,1,0:T(2,128)(2,1)} %reshape.279), calls=%async_computation | async-start | bytes 1048576 | tf_op jit(solution)/shard_map/all_to_all | solution.py:102
  49.3 714.7 %reduce-scatter.2.cloned.1.call-start = ((), (), s32[]{:S(2)}) async-start(), calls=%async_computation.4 | async-start | bytes 4259840 | tf_op jit(solution)/shard_map/reduce_scatter | solution.py:109
  207.9 149.2 %copy-start.19 = (f32[1024]{0:T(1024)}, f32[1024]{0:T(1024)S(1)}, u32[]{:S(2)}) copy-start(f32[1024]{0:T(1024)S(1)} %all-reduce.3) | copy-start | bytes 12292
  357.9 5.6 copy-start.15
  361.3 9.4 %copy-start.23 = (f32[256]{0:T(256)}, f32[256]{0:T(256)S(1)}, u32[]{:S(2)}) copy-start(f32[256]{0:T(256)S(1)} %get-tuple-element.24) | copy-start | bytes 3076
  365.0 0.8 copy-start.6
  384.8 4.0 copy-start.24
  393.3 0.7 copy-start.22
  401.7 2.7 copy-start.5
  404.4 7.7 copy-start.17
  404.4 141.6 %copy-start.20 = (f32[1024]{0:T(1024)S(1)}, f32[1024]{0:T(1024)}, u32[]{:S(2)}) copy-start(f32[1024]{0:T(1024)} %copy-done.19) | copy-start | bytes 12292
  407.2 296.4 %all-to-all-start.1 = ((bf16[64,4,1024]{2,1,0:T(4,128)(2,1)}), bf16[64,4,1024]{2,1,0:T(4,128)(2,1)S(1)}, u32[]{:S(2)}, u32[]{:S(2)}) async-start(bf16[64,4,1024]{2,1,0:T(4,128)(2,1)} %fusion.47), calls=%async_computation.1 | async-start | bytes 1048576 | tf_op jit(solution)/shard_map/all_to_all | solution.py:106
  412.0 436.7 %all-reduce.6.cloned.1.call-start = ((), (), s32[]{:S(2)}) async-start(), calls=%async_computation.5 | async-start | bytes 131072 | tf_op jit(solution)/shard_map/psum | solution.py:110
  704.6 3.9 copy-start.10
  708.5 2.4 copy-start.2
  710.8 1.2 copy-start.4
  710.8 1.7 copy-start.12
  712.5 1.2 copy-start.13
  712.5 2.4 slice-start
  713.8 1.5 copy-start.8
  713.8 2.2 slice-start.1
  713.8 2.2 copy-start.30
  716.0 2.9 copy-start.26
  716.0 48.0 %copy-start.14 = (bf16[256,1024]{1,0:T(8,128)(2,1)S(1)}, bf16[256,1024]{1,0:T(8,128)(2,1)}, u32[]{:S(2)}) copy-start(bf16[256,1024]{1,0:T(8,128)(2,1)} %squeeze.21) | copy-start | bytes 1572868
  716.0 48.0 %copy-start.29 = (f32[256]{0:T(256)S(1)}, f32[256]{0:T(256)}, u32[]{:S(2)}) copy-start(f32[256]{0:T(256)} %copy-done.28) | copy-start | bytes 3076
Sparse Core Ops, SparseCore 0:
  12.1 128.8 all-gather.2
  393.4 370.5 reduce-scatter.1
  766.8 81.8 all-reduce.5
where the time goes:
time: 858 us; the launch traced here: 857 us
  blocking collectives  593 us (69%)
  waiting for transfers between devices  128 us (15%)
  matrix products  45.3 us (5%)
  local copies, waits for them, and re-layouts  30.5 us (4%)
  other arithmetic  24.6 us (3%)
  starting transfers between devices  20.1 us (2%)
  between operations  15.7 us (2%)
    unnamed x1, blocking collectives  157 us
    psum x1, blocking collectives, per_device(): mixed_err = lax.psum(jnp.sum(u_wide * w_v, axis=0), 'tm')  156 us
    all_gather x1, blocking collectives, per_device(): z = lax.all_gather(z, 'tm', axis=0, tiled=True)  148 us
    psum x1, blocking collectives, per_device(): u_mine = lax.psum(u_terms, ('env', 'tm'))  132 us
    psum x1, waiting for transfers between devices, per_device(): qk_grad = lax.psum(summed, 'env').astype(jnp.float32)  82.4 us
    reduce_scatter x1, waiting for transfers between devices, per_device(): summed = lax.psum_scatter(terms, 'tm', scatter_dimension=0, tiled=True)  45.1 us
  transfers between devices with their start and end apart: 5, of which 2 were waited for; matrix products, arithmetic and copies ran while one was open for 8% of the time, Pallas kernels for 0%

commit v1 on v0

--- a/solution.py
+++ b/solution.py
@@ -107,7 +107,8 @@
     terms = left_product(normed, dqk).astype(jnp.bfloat16)
     u_terms = lax.dot_general(normed.astype(jnp.float32), t, (((0,), (0,)), ((), ())), precision=HI)
     summed = lax.psum_scatter(terms, "tm", scatter_dimension=0, tiled=True)
-    qk_grad = lax.psum(summed, "env").astype(jnp.float32)
+    run_axis_part = lambda content, which_axis: jnp.sum(lax.all_gather(content, which_axis), axis=0)
+    qk_grad = run_axis_part(summed, "env").astype(jnp.float32)
     u_mine = lax.psum(u_terms, ("env", "tm"))
     u_mine = lax.dynamic_slice_in_dim(u_mine, lax.axis_index("tm") * w_v.shape[0], w_v.shape[0], 0)
     u_wide = jnp.repeat(u_mine, size, axis=1)

time: 858 us -> 828 us (0.965)
  waiting for transfers between devices: 128 us -> 45.1 us
  blocking collectives: 593 us -> 648 us
    psum x1 -> x0, waiting for transfers between devices: 82.4 us -> none  [per_device(): qk_grad = lax.psum(summed, 'env').astype(jnp.float32)]
    all_gather x0 -> x1, blocking collectives: none -> 55 us  [per_device(): lax.all_gather(content, which_axis)]
  transfers between devices with their start and end apart: 5 -> 4, of which waited for: 2 -> 1; matrix products, arithmetic and copies ran while one was open for 8% -> 8% of each run, Pallas kernels for 0% -> 0%
where the time goes in v1:
time: 828 us; the launch traced here: 826 us
  blocking collectives  648 us (78%)
  waiting for transfers between devices  45.1 us (5%)
  matrix products  44.4 us (5%)
  local copies, waits for them, and re-layouts  30.4 us (4%)
  other arithmetic  22.6 us (3%)
  starting transfers between devices  20.1 us (2%)
  between operations  16 us (2%)
    unnamed x1, blocking collectives  157 us
    psum x1, blocking collectives, per_device(): mixed_err = lax.psum(jnp.sum(u_wide * w_v, axis=0), 'tm')  155 us
    all_gather x1, blocking collectives, per_device(): z = lax.all_gather(z, 'tm', axis=0, tiled=True)  148 us
    psum x1, blocking collectives, per_device(): u_mine = lax.psum(u_terms, ('env', 'tm'))  132 us
    all_gather x1, blocking collectives, per_device(): lax.all_gather(content, which_axis)  55 us
    reduce_scatter x1, waiting for transfers between devices, per_device(): summed = lax.psum_scatter(terms, 'tm', scatter_dimension=0, tiled=True)  45.1 us
  transfers between devices with their start and end apart: 4, of which 1 were waited for; matrix products, arithmetic and copies ran while one was open for 8% of the time, Pallas kernels for 0%

profile of v1, /device:TPU:1, one launch (start us, length us, event | category | flops | bytes accessed | tf_op | source)
XLA Modules:
  0.0 826.2 jit_solution(10811044870625928464)
XLA Ops:
  7.2 1.6 slice.24
  9.5 1.2 fusion.49
  10.7 0.5 copy-done.25
  11.3 4.9 convolution_convert_fusion
  16.1 1.1 slice_bitcast_fusion
  17.2 1.4 copy.98
  18.7 2.2 copy.97
  21.0 1.6 fusion.114
  23.3 0.7 copy-done.1
  24.0 1.0 copy-done.3
  25.4 0.7 fusion.37
  26.1 0.8 copy.135
  27.0 0.5 broadcast.202
  27.5 4.5 reduce.5
  32.0 2.2 reshape.280
  34.2 15.1 %all-to-all-start = ((bf16[64,2,2048]{2,1,0:T(2,128)(2,1)}), bf16[64,2,2048]{2,1,0:T(2,128)(2,1)S(1)}, u32[]{:S(2)}, u32[]{:S(2)}) async-start(bf16[64,2,2048]{2,1,0:T(2,128)(2,1)} %reshape.280), calls=%async_computation | async-start | bytes 1048576 | tf_op jit(solution)/shard_map/all_to_all | solution.py:102
  49.4 0.6 dynamic-slice
  51.0 156.9 %all-reduce.3 = f32[1024]{0:T(1024)S(1)} all-reduce(f32[1024]{0:T(1024)S(1)} %dynamic-update-slice), channel_id=1, replica_groups=mesh['env'=4,'tm'=64] {'tm'}, use_global_device_ids=true, to_apply=%add.3 | all-reduce | flops 1024 | bytes 8192
  207.9 0.8 fusion.93
  208.9 148.0 %all-gather.1 = f32[64,16,8]{1,2,0:T(8,128)S(1)} all-gather(f32[1,16,8]{1,2,0:T(8,128)S(1)} %bitcast.171), channel_id=1, replica_groups=mesh['env'=4,'tm'=64] {'tm'}, dimensions={0}, use_global_device_ids=true | all-gather | bytes 33280 | tf_op jit(solution)/shard_map/all_gather | solution.py:97
  357.2 0.7 broadcast_or_fusion
  357.9 1.8 reshape.281
  359.7 1.6 fusion.39
  361.5 0.7 copy.75
  362.2 1.3 reshape.268
  363.5 1.5 multiply_convert_fusion
  365.0 0.8 copy-done.6
  365.8 1.3 convolution_bitcast_fusion.3
  367.1 3.5 fusion.16
  370.9 1.0 fusion.113
  371.9 3.5 multiply_reduce_fusion.2
  375.4 1.3 fusion.95
  376.7 3.3 convolution_bitcast_fusion
  380.0 3.4 convolution_bitcast_fusion.1
  383.5 1.3 maximum_convert_fusion
  384.8 1.7 copy.78
  386.4 2.3 convert_element_type.175
  388.7 4.6 convolution_convert_fusion.1
  393.5 0.5 copy-done.22
  394.1 1.6 multiply_reduce_fusion
  395.8 3.8 fusion.115
  399.6 2.1 fusion.40
  401.8 2.6 reshape.260
  404.4 2.8 fusion.47
  407.2 4.9 all-to-all-start.1
  412.1 1.5 convolution_bitcast_fusion.2
  413.5 132.3 %psum.14 = f32[1024,8]{0,1:T(8,128)S(1)} all-reduce(f32[1024,8]{0,1:T(8,128)S(1)} %convolution_bitcast_fusion.2), channel_id=1, replica_groups=mesh['env'=4,'tm'=64] {'env','tm'}, use_global_device_ids=true, to_apply=%region_19.20 | all-reduce | flops 8192 | bytes 65536 | tf_op jit(solution)/shard_map/psum | solution.py:112
  546.0 0.8 fusion.94
  546.8 155.3 %psum.15 = f32[1024]{0:T(1024)S(1)} all-reduce(f32[1024]{0:T(1024)S(1)} %get-tuple-element.19), channel_id=1, replica_groups=mesh['env'=4,'tm'=64] {'tm'}, use_global_device_ids=true, to_apply=%region_21.22 | all-reduce | flops 1024 | bytes 8192 | tf_op jit(solution)/shard_map/psum | solution.py:116
  702.2 0.7 broadcast_multiply_fusion
  702.9 0.9 squeeze.21
  703.9 2.7 convolution_convert_fusion.5
  706.5 1.2 copy.94
  707.8 2.3 fusion.6
  710.2 1.0 convert_reduce_fusion
  711.4 0.5 convolution_convert_fusion.4
  711.9 1.2 fusion.25
  713.1 1.2 fusion.24
  714.6 0.7 slice-done.1
  715.3 2.0 fusion.52
  717.3 1.1 fusion.67
  718.5 45.1 %reduce-scatter.2.cloned.1.call-done = bf16[16,2048]{1,0:T(8,128)(2,1)} async-done(((bf16[1024,2048]{1,0:T(8,128)(2,1)}), bf16[16,2048]{1,0:T(8,128)(2,1)}) %reduce-scatter.2.cloned.1.call-update) | async-done | bytes 65552 | tf_op jit(solution)/shard_map/reduce_scatter | solution.py:109
  763.6 55.0 %all-gather = bf16[64,2048]{1,0:T(8,128)(2,1)S(1)} all-gather(bf16[16,2048]{1,0:T(8,128)(2,1)} %reduce-scatter.2.cloned.1.call-done), channel_id=2, replica_groups=mesh['env'=4,'tm'=64] {'env'}, dimensions={0}, use_global_device_ids=true | all-gather | bytes 327680 | tf_op jit(solution)/shard_map/all_gather | solution.py:110
  818.7 0.7 pad_maximum_fusion
  (106 shorter events, 3.9 us)
Async XLA Ops:
  7.2 18.2 %copy-start = (bf16[1024,1024]{1,0:T(8,128)(2,1)S(1)}, bf16[1024,1024]{1,0:T(8,128)(2,1)}, u32[]{:S(2)}) copy-start(bf16[1024,1024]{1,0:T(8,128)(2,1)} %param.17) | copy-start | bytes 6291460
  7.2 359.9 %all-gather.4.cloned.1.call-start = ((), (), s32[]{:S(2)}) async-start(), calls=%async_computation.3 | async-start | bytes 4259840 | tf_op jit(solution)/shard_map/all_gather | solution.py:98
  10.7 0.5 copy-start.25
  11.3 4.9 copy-start.28
  17.2 6.8 copy-start.9
  18.7 3.9 copy-start.11
  22.6 1.4 copy-start.1
  22.9 2.4 copy-start.16
  22.9 2.4 copy-start.7
  24.0 1.0 copy-start.3
  26.9 22.4 %copy-start.31 = (u32[256]{0:T(256)S(1)}, u32[256]{0:T(256)}, u32[]{:S(2)}) copy-start(u32[256]{0:T(256)} %constant.62) | copy-start | bytes 3076
  26.9 23.7 %copy-start.18 = (f32[1024]{0:T(1024)S(1)}, f32[1024]{0:T(1024)}, u32[]{:S(2)}) copy-start(f32[1024]{0:T(1024)} %param.21) | copy-start | bytes 12292
  27.0 23.7 %copy-start.21 = (bf16[16,1024]{1,0:T(8,128)(2,1)S(1)}, bf16[16,1024]{1,0:T(8,128)(2,1)}, u32[]{:S(2)}) copy-start(bf16[16,1024]{1,0:T(8,128)(2,1)} %param.20) | copy-start | bytes 98308
  32.0 325.1 %copy-start.27 = (s32[1,64,4]{1,2,0:T(4,128)S(1)}, s32[1,64,4]{1,2,0:T(4,128)}, u32[]{:S(2)}) copy-start(s32[1,64,4]{1,2,0:T(4,128)} %param.13) | copy-start | bytes 3076
  34.2 323.7 %all-to-all-start = ((bf16[64,2,2048]{2,1,0:T(2,128)(2,1)}), bf16[64,2,2048]{2,1,0:T(2,128)(2,1)S(1)}, u32[]{:S(2)}, u32[]{:S(2)}) async-start(bf16[64,2,2048]{2,1,0:T(2,128)(2,1)} %reshape.280), calls=%async_computation | async-start | bytes 1048576 | tf_op jit(solution)/shard_map/all_to_all | solution.py:102
  49.3 714.3 %reduce-scatter.2.cloned.1.call-start = ((), (), s32[]{:S(2)}) async-start(), calls=%async_computation.4 | async-start | bytes 4259840 | tf_op jit(solution)/shard_map/reduce_scatter | solution.py:109
  207.9 149.2 %copy-start.19 = (f32[1024]{0:T(1024)}, f32[1024]{0:T(1024)S(1)}, u32[]{:S(2)}) copy-start(f32[1024]{0:T(1024)S(1)} %all-reduce.3) | copy-start | bytes 12292
  357.9 5.6 copy-start.15
  361.3 9.4 %copy-start.23 = (f32[256]{0:T(256)}, f32[256]{0:T(256)S(1)}, u32[]{:S(2)}) copy-start(f32[256]{0:T(256)S(1)} %get-tuple-element.24) | copy-start | bytes 3076
  365.0 0.8 copy-start.6
  384.8 4.0 copy-start.24
  393.3 0.7 copy-start.22
  401.7 2.7 copy-start.5
  404.4 7.7 copy-start.17
  404.4 141.6 %copy-start.20 = (f32[1024]{0:T(1024)S(1)}, f32[1024]{0:T(1024)}, u32[]{:S(2)}) copy-start(f32[1024]{0:T(1024)} %copy-done.19) | copy-start | bytes 12292
  407.2 295.8 %all-to-all-start.1 = ((bf16[64,4,1024]{2,1,0:T(4,128)(2,1)}), bf16[64,4,1024]{2,1,0:T(4,128)(2,1)S(1)}, u32[]{:S(2)}, u32[]{:S(2)}) async-start(bf16[64,4,1024]{2,1,0:T(4,128)(2,1)} %fusion.47), calls=%async_computation.1 | async-start | bytes 1048576 | tf_op jit(solution)/shard_map/all_to_all | solution.py:106
  703.9 3.9 copy-start.10
  707.8 2.4 copy-start.2
  710.1 1.2 copy-start.4
  710.2 1.7 copy-start.12
  711.9 1.2 copy-start.13
  711.9 2.4 slice-start
  713.1 1.5 copy-start.8
  713.1 2.2 slice-start.1
  713.1 2.2 copy-start.30
  715.3 2.0 copy-start.26
  715.3 2.0 copy-start.14
  715.3 2.0 copy-start.29
Sparse Core Ops, SparseCore 0:
  12.1 128.8 all-gather.3
  393.4 370.0 reduce-scatter.1
